TPU v7x, 32 devices: a whole 2x2x4 slice. The times are simulated.
32 devices in a mesh: group: 2 (over y), seq: 4 (over z), doc: 4 (over x, core).
Axes of the slice: x: 2, y: 2, z: 4, core: 2. Of those that a mesh axis runs over, the one named last changes fastest.
Arguments:
- query_vectors: bfloat16 [8, 512, 1024], P(('group', 'doc'), 'seq'), parts along dimension 0, may hold values from -6 to 6
- key_vectors: bfloat16 [8, 512, 1024], P(('group', 'doc'), 'seq'), parts along dimension 0, may hold values from -6 to 6
- value_vectors: bfloat16 [8, 512, 1024], P(('group', 'doc'), 'seq'), parts along dimension 0, may hold values from -6 to 6
- out_grad: bfloat16 [8, 512, 1024], P(('group', 'doc'), 'seq'), parts along dimension 0, may hold values from -6 to 6
- pad_length: int32 [8], P(('group', 'doc')), parts along dimension 0, may hold values from 1 to 256
Outputs:
- attended: bfloat16 [8, 512, 1024], P(('group', 'doc'), 'seq'), parts along dimension 0
- query_grad: bfloat16 [8, 512, 1024], P(('group', 'doc'), 'seq'), parts along dimension 0
- key_grad: bfloat16 [8, 512, 1024], P(('group', 'doc'), 'seq'), parts along dimension 0
- value_grad: bfloat16 [8, 512, 1024], P(('group', 'doc'), 'seq'), parts along dimension 0
There are 2 independent parts, one for each index of `group`. A program takes and returns all parts, laid end to end along the dimension named above; each array names one. Nothing has to cross between parts.
All inputs are finite; a program needn't handle non-finite values.
Results may differ from a plain program's by a relative error of at most 0.015.
Values may be sent and summed in bfloat16 or wider, within the bound.
A program may use at most 64 MiB of HBM per device.

v0:
```python
import math

import jax
import jax.numpy as jnp
from jax import lax
from jax.sharding import PartitionSpec as P

D = 1024
H = 16
W = 128
G = 64


very_negative = -1e30


def broadcast(block, axis, owner):
    block = jnp.where(lax.axis_index(axis) == owner, block, jnp.zeros_like(block))
    return lax.psum(block, axis)


def extended(block, sides, width):
    for axis, dim in sides:
        count = lax.axis_size(axis)
        forward = [(i, i + 1) for i in range(count - 1)]
        backward = [(target, source) for source, target in forward]
        low = lax.ppermute(
            lax.slice_in_dim(block, block.shape[dim] - width, None, axis=dim), axis, forward
        )
        high = lax.ppermute(lax.slice_in_dim(block, 0, width, axis=dim), axis, backward)
        block = jnp.concatenate([low, block, high], axis=dim)
    return block


def shifted(block, axis, distance):
    devices = range(lax.axis_size(axis))
    route = [(i - distance, i) for i in devices if i - distance in devices]
    return lax.ppermute(block, axis, route)


def split_heads(block_rows, head_size):
    return block_rows.reshape(block_rows.shape[0], -1, head_size)


def join_heads(block_rows):
    return block_rows.reshape(block_rows.shape[0], -1)


def band_terms(query_rows, grad_rows, key_all, value_all, allowed, row_live, head_size):
    score_scale = 1.0 / math.sqrt(head_size)
    query_heads = split_heads(query_rows, head_size)
    grad_heads = split_heads(grad_rows, head_size)
    key_heads = split_heads(key_all, head_size)
    value_heads = split_heads(value_all, head_size)
    scores = (
        jnp.einsum("qhd,khd->hqk", query_heads, key_heads, preferred_element_type=jnp.float32)
        * score_scale
    )
    scores = jnp.where(allowed[None], scores, very_negative)
    largest = jnp.max(scores, axis=2, keepdims=True)
    expo = jnp.where(allowed[None], jnp.exp(scores - largest), 0.0)
    totals = jnp.sum(expo, axis=2, keepdims=True)
    probs = expo / totals
    log_total = (largest + jnp.log(totals))[:, :, 0]
    probs_low = probs.astype(jnp.bfloat16)
    attn = jnp.einsum("hqk,khd->qhd", probs_low, value_heads, preferred_element_type=jnp.float32)
    delta = jnp.sum(grad_heads.astype(jnp.float32) * attn, axis=2).T
    dprob = jnp.einsum("qhd,khd->hqk", grad_heads, value_heads, preferred_element_type=jnp.float32)
    keep_rows = row_live[None, :, None]
    dscore = jnp.where(keep_rows, probs * (dprob - delta[:, :, None]), 0.0).astype(jnp.bfloat16)
    kept_low = jnp.where(keep_rows, probs_low, jnp.zeros_like(probs_low))
    query_grad = (
        jnp.einsum("hqk,khd->qhd", dscore, key_heads, preferred_element_type=jnp.float32)
        * score_scale
    )
    key_grad = (
        jnp.einsum("hqk,qhd->khd", dscore, query_heads, preferred_element_type=jnp.float32)
        * score_scale
    )
    value_grad = jnp.einsum(
        "hqk,qhd->khd", kept_low, grad_heads, preferred_element_type=jnp.float32
    )
    return (
        join_heads(attn),
        log_total,
        delta,
        join_heads(query_grad),
        join_heads(key_grad),
        join_heads(value_grad),
    )


def place_suffix(suffix_rows, row_count):
    return jnp.pad(suffix_rows, ((row_count - G, 0), (0, 0)))


def per_device(query_vectors, key_vectors, value_vectors, out_grad, pad_length):
    query_local = query_vectors[0]
    key_local = key_vectors[0]
    value_local = value_vectors[0]
    grad_local = out_grad[0]
    row_count = query_local.shape[0]
    feature_count = query_local.shape[1]
    head_size = D // H
    score_scale = 1.0 / math.sqrt(head_size)
    seq_count = lax.axis_size("seq")
    seq_rank = lax.axis_index("seq")
    suffix_start = row_count * seq_count - G
    valid_end = suffix_start - pad_length[0]
    first_row = seq_rank * row_count
    query_pos = first_row + jnp.arange(row_count, dtype=jnp.int32)
    window_pos = first_row - W + jnp.arange(row_count + 2 * W, dtype=jnp.int32)
    row_live = query_pos < suffix_start
    row_suffix = query_pos >= suffix_start
    suffix_block = jnp.stack(
        [
            query_local[row_count - G :],
            key_local[row_count - G :],
            value_local[row_count - G :],
            grad_local[row_count - G :],
        ]
    )
    suffix_block = broadcast(suffix_block, "seq", seq_count - 1)
    query_glob = suffix_block[0]
    key_glob = suffix_block[1]
    value_glob = suffix_block[2]
    grad_glob = suffix_block[3]
    border = extended(jnp.stack([key_local, value_local]), (("seq", 1),), W)
    key_all = jnp.concatenate([border[0], key_glob], axis=0)
    value_all = jnp.concatenate([border[1], value_glob], axis=0)
    within = (
        (jnp.abs(query_pos[:, None] - window_pos[None, :]) <= W)
        & (window_pos >= 0)[None, :]
        & (window_pos < valid_end)[None, :]
    )
    allowed = jnp.concatenate([within, jnp.ones((row_count, G), dtype=bool)], axis=1)
    heads_per = min(4, H)
    group_width = heads_per * head_size
    group_terms = []
    for column in range(0, feature_count, group_width):
        columns = slice(column, column + group_width)
        group_terms.append(
            band_terms(
                query_local[:, columns],
                grad_local[:, columns],
                key_all[:, columns],
                value_all[:, columns],
                allowed,
                row_live,
                head_size,
            )
        )
    attn_band = jnp.concatenate([terms[0] for terms in group_terms], axis=1)
    query_band = jnp.concatenate([terms[3] for terms in group_terms], axis=1)
    key_tail = jnp.concatenate([terms[4] for terms in group_terms], axis=1)
    value_tail = jnp.concatenate([terms[5] for terms in group_terms], axis=1)
    local_live = (query_pos < valid_end) | row_suffix
    query_gh = split_heads(query_glob, head_size)
    grad_gh = split_heads(grad_glob, head_size)
    key_heads = split_heads(key_local, head_size)
    value_heads = split_heads(value_local, head_size)
    gscores = (
        jnp.einsum("ghd,khd->hgk", query_gh, key_heads, preferred_element_type=jnp.float32)
        * score_scale
    )
    gscores = jnp.where(local_live[None, None, :], gscores, very_negative)
    glob_top = lax.pmax(jnp.max(gscores, axis=2), "seq")
    weights = jnp.where(local_live[None, None, :], jnp.exp(gscores - glob_top[:, :, None]), 0.0)
    weight_sums = jnp.sum(weights, axis=2)
    weighted = join_heads(
        jnp.einsum(
            "hgk,khd->ghd",
            weights.astype(jnp.bfloat16),
            value_heads,
            preferred_element_type=jnp.float32,
        )
    )
    weight_sums, weighted = lax.psum((weight_sums, weighted), "seq")
    attn_glob = split_heads(weighted, head_size) / weight_sums.T[:, :, None]
    log_glob = glob_top + jnp.log(weight_sums)
    delta_glob = jnp.sum(grad_gh.astype(jnp.float32) * attn_glob, axis=2).T
    gprobs = jnp.where(local_live[None, None, :], jnp.exp(gscores - log_glob[:, :, None]), 0.0)
    gdprob = jnp.einsum("ghd,khd->hgk", grad_gh, value_heads, preferred_element_type=jnp.float32)
    gdscore = (gprobs * (gdprob - delta_glob[:, :, None])).astype(jnp.bfloat16)
    query_part = (
        join_heads(
            jnp.einsum("hgk,khd->ghd", gdscore, key_heads, preferred_element_type=jnp.float32)
        )
        * score_scale
    )
    key_add = (
        join_heads(
            jnp.einsum("hgk,ghd->khd", gdscore, query_gh, preferred_element_type=jnp.float32)
        )
        * score_scale
    )
    value_add = join_heads(
        jnp.einsum(
            "hgk,ghd->khd", gprobs.astype(jnp.bfloat16), grad_gh, preferred_element_type=jnp.float32
        )
    )
    suffix_terms = jnp.stack(
        [query_part, key_tail[key_tail.shape[0] - G :], value_tail[value_tail.shape[0] - G :]]
    )
    query_sum, key_sum, value_sum = lax.psum(
        (suffix_terms[0], suffix_terms[1], suffix_terms[2]), "seq"
    )
    outgoing = jnp.stack([key_tail[:W], value_tail[:W]])
    incoming = jnp.stack(
        [key_tail[W + row_count : 2 * W + row_count], value_tail[W + row_count : 2 * W + row_count]]
    )
    from_after = shifted(outgoing.astype(jnp.bfloat16), "seq", -1).astype(outgoing.dtype)
    from_before = shifted(incoming.astype(jnp.bfloat16), "seq", 1).astype(incoming.dtype)
    key_band = key_tail[W : W + row_count] + from_after[0] + from_before[0]
    value_band = value_tail[W : W + row_count] + from_after[1] + from_before[1]
    suffix_mask = row_suffix[:, None]
    attended = jnp.where(suffix_mask, place_suffix(join_heads(attn_glob), row_count), attn_band)
    query_total = query_band + jnp.where(suffix_mask, place_suffix(query_sum, row_count), 0.0)
    key_total = key_band + key_add + jnp.where(suffix_mask, place_suffix(key_sum, row_count), 0.0)
    value_total = (
        value_band + value_add + jnp.where(suffix_mask, place_suffix(value_sum, row_count), 0.0)
    )
    return (
        attended.astype(jnp.bfloat16)[None],
        query_total.astype(jnp.bfloat16)[None],
        key_total.astype(jnp.bfloat16)[None],
        value_total.astype(jnp.bfloat16)[None],
    )


def solution(mesh):
    return jax.shard_map(
        per_device,
        mesh=mesh,
        in_specs=(
            P(("group", "doc"), "seq", None),
            P(("group", "doc"), "seq", None),
            P(("group", "doc"), "seq", None),
            P(("group", "doc"), "seq", None),
            P(("group", "doc")),
        ),
        out_specs=(
            P(("group", "doc"), "seq", None),
            P(("group", "doc"), "seq", None),
            P(("group", "doc"), "seq", None),
            P(("group", "doc"), "seq", None),
        ),
        check_vma=False,
    )
```

profile of v0, /device:TPU:0, one launch (start us, length us, event | category | flops | bytes accessed | tf_op | source)
XLA Modules:
  0.0 221.9 jit_solution(294880592946299408)
XLA Ops:
  7.3 1.1 constant_dynamic-update-slice_fusion.1
  8.4 1.0 constant_dynamic-update-slice_fusion
  9.4 1.3 collective-permute-start.1
  10.7 5.6 %collective-permute-start = (bf16[2,128,1024]{2,1,0:T(8,128)(2,1)S(1)}, bf16[2,128,1024]{2,1,0:T(8,128)(2,1)S(1)}, u32[]{:S(2)}, u32[]{:S(2)}) collective-permute-start(bf16[2,128,1024]{2,1,0:T(8,128)(2,1)S(1)} %constant_dynamic-update-slice_fusion), channel_id=1, source_target_pairs={{0,4},{4,8},{8,12},{1,5},{5,9},{9,13},{2,6},{6,10},{10,14},{3,7},{... | collective-permute-start | bytes 1572872 | tf_op jit(solution)/shard_map/ppermute | solution.py:27
  16.4 0.9 maximum_select_fusion
  18.4 0.7 copy.113
  20.6 0.7 copy.114
  21.3 0.7 copy.99
  22.1 0.7 copy.108
  25.7 3.1 %collective-permute-done.1 = bf16[2,128,1024]{2,1,0:T(8,128)(2,1)S(1)} collective-permute-done((bf16[2,128,1024]{2,1,0:T(8,128)(2,1)S(1)}, bf16[2,128,1024]{2,1,0:T(8,128)(2,1)S(1)}, u32[]{:S(2)}, u32[]{:S(2)}) %collective-permute-start.1) | collective-permute-done | bytes 524320 | tf_op jit(solution)/shard_map/ppermute | solution.py:30
  28.8 3.8 %collective-permute-done = bf16[2,128,1024]{2,1,0:T(8,128)(2,1)S(1)} collective-permute-done((bf16[2,128,1024]{2,1,0:T(8,128)(2,1)S(1)}, bf16[2,128,1024]{2,1,0:T(8,128)(2,1)S(1)}, u32[]{:S(2)}, u32[]{:S(2)}) %collective-permute-start) | collective-permute-done | bytes 524320 | tf_op jit(solution)/shard_map/ppermute | solution.py:27
  32.8 26.0 %all-reduce.10.cloned.1.call-done = bf16[4,64,1024]{2,1,0:T(8,128)(2,1)} async-done(((bf16[4,64,1024]{2,1,0:T(8,128)(2,1)}), bf16[4,64,1024]{2,1,0:T(8,128)(2,1)}) %all-reduce.10.cloned.1.call-update) | async-done | bytes 524304 | tf_op jit(solution)/shard_map/psum | solution.py:19
  58.8 1.8 fusion.126
  60.6 0.9 fusion.89
  61.5 1.1 copy.104
  62.6 1.1 copy.103
  63.7 1.5 fusion.130
  65.3 0.9 fusion.101
  66.5 0.9 convolution_multiply_fusion.12
  67.7 1.1 fusion.58
  69.2 1.5 fusion.129
  70.6 1.3 fusion.74
  72.0 0.9 fusion.100
  73.2 0.9 convolution_multiply_fusion.11
  74.4 1.1 fusion.56
  75.9 1.5 fusion.131
  77.4 1.3 fusion.72
  78.7 0.9 fusion.102
  79.9 0.9 convolution_multiply_fusion.13
  81.2 1.1 fusion.60
  83.3 1.5 fusion.132
  84.8 1.3 fusion.71
  86.2 0.9 fusion.103
  87.0 1.1 fusion.62
  89.6 1.5 pad_maximum_fusion
  91.1 1.3 copy.130
  92.4 1.2 copy.131
  93.8 1.2 copy.128
  95.1 1.1 fusion.124
  96.2 1.5 pad_maximum_fusion.1
  98.2 11.0 %pmax.7 = f32[16,64]{1,0:T(8,128)S(1)} all-reduce(f32[16,64]{1,0:T(8,128)S(1)} %get-tuple-element.44), channel_id=1, replica_groups=mesh['group'=2,'seq'=4,'doc'=4] {'seq'}, use_global_device_ids=true, to_apply=%region_2.3 | all-reduce | flops 1024 | bytes 8192 | tf_op jit(solution)/shard_map/pmax | solution.py:167
  109.6 8.7 %psum.44 = f32[16,64]{1,0:T(8,128)S(1)} all-reduce(f32[16,64]{1,0:T(8,128)S(1)} %fusion.68), channel_id=1, replica_groups=mesh['group'=2,'seq'=4,'doc'=4] {'seq'}, use_global_device_ids=true, to_apply=%region_5.6 | all-reduce | flops 1024 | bytes 8192 | tf_op jit(solution)/shard_map/psum | solution.py:178
  118.7 1.1 copy.95
  119.8 1.9 reshape.185
  121.8 0.7 slice_bitcast_fusion.9
  122.5 0.7 slice_bitcast_fusion.8
  123.2 0.8 pad_maximum_fusion.4
  124.7 1.7 slice.193
  126.3 1.7 slice.197
  128.0 4.6 %collective-permute-start.3 = (bf16[2,128,1024]{2,1,0:T(8,128)(2,1)}, bf16[2,128,1024]{2,1,0:T(8,128)(2,1)}, u32[]{:S(2)}, u32[]{:S(2)}) collective-permute-start(bf16[2,128,1024]{2,1,0:T(8,128)(2,1)} %pad_maximum_fusion.4), channel_id=1, source_target_pairs={{0,4},{4,8},{8,12},{1,5},{5,9},{9,13},{2,6},{6,10},{10,14},{3,7},{... | collective-permute-start | bytes 1572872 | tf_op jit(solution)/shard_map/ppermute | solution.py:38
  133.0 24.8 %all-reduce.12.cloned.1.call-done = f32[64,1024]{1,0:T(8,128)} async-done(((f32[64,1024]{1,0:T(8,128)}), f32[64,1024]{1,0:T(8,128)}) %all-reduce.12.cloned.1.call-update) | async-done | bytes 262160 | tf_op jit(solution)/shard_map/psum | solution.py:178
  157.8 1.1 reshape.210
  160.4 0.9 mul.169
  161.3 0.8 pad_maximum_fusion.3
  162.2 1.4 collective-permute-start.2
  163.6 0.9 convolution_multiply_fusion.14
  165.6 1.0 copy.118
  166.7 0.8 copy.117
  168.1 0.8 fusion.82
  168.9 1.1 convert_element_type.95
  170.1 19.5 %collective-permute-done.2 = bf16[2,128,1024]{2,1,0:T(8,128)(2,1)} collective-permute-done((bf16[2,128,1024]{2,1,0:T(8,128)(2,1)}, bf16[2,128,1024]{2,1,0:T(8,128)(2,1)}, u32[]{:S(2)}, u32[]{:S(2)}) %collective-permute-start.2) | collective-permute-done | bytes 524320 | tf_op jit(solution)/shard_map/ppermute | solution.py:38
  189.6 1.1 convert_element_type.94
  190.8 22.0 %all-reduce.14.cloned.1.call-done = (f32[64,1024]{1,0:T(8,128)}, f32[64,1024]{1,0:T(8,128)}, f32[64,1024]{1,0:T(8,128)}) async-done(((f32[64,1024]{1,0:T(8,128)}, f32[64,1024]{1,0:T(8,128)}, f32[64,1024]{1,0:T(8,128)}), (f32[64,1024]{1,0:T(8,128)}, f32[64,1024]{1,0:T(8,128)}, f32[64,1024]{1,0:T(8,128)})) %all-reduce.14.cloned.1.call-update) | async-done | bytes 786448 | tf_op jit(solution)/shard_map/psum | solution.py:205
  212.8 2.7 %fusion.84 = (bf16[1,128,1024]{2,1,0:T(8,128)(2,1)}, bf16[1,128,1024]{2,1,0:T(8,128)(2,1)}, bf16[1,128,1024]{2,1,0:T(8,128)(2,1)}) fusion(f32[64,1024]{1,0:T(8,128)} %get-tuple-element.6, f32[128,1024]{1,0:T(8,128)S(1)} %copy.135, f32[2,128,1024]{2,1,0:T(8,128)S(1)} %convert_element_type.95, f32[2,128,1024]{2,1,0:T(8,128)S(1)} %convert_element_type.94, ...), kind=kLoop, calls=%fused_computation.140 | loop fusion | flops 2359296 | bytes 6291584 | tf_op jit(solution)/shard_map/broadcast_in_dim | solution.py:227
  (159 shorter events, 15.9 us)
Async XLA Ops:
  7.2 9.1 %slice-start = ((bf16[1,128,1024]{2,1,0:T(8,128)(2,1)}), bf16[1,64,1024]{2,1,0:T(8,128)(2,1)S(1)}, s32[]{:S(2)}) async-start(bf16[1,128,1024]{2,1,0:T(8,128)(2,1)} %param.6), calls=%async_computation.3 | async-start | bytes 262144 | tf_op jit(solution)/shard_map/slice | solution.py:118
  7.2 10.2 %copy-start.4 = (bf16[1,128,1024]{2,1,0:T(8,128)(2,1)S(1)}, bf16[1,128,1024]{2,1,0:T(8,128)(2,1)}, u32[]{:S(2)}) copy-start(bf16[1,128,1024]{2,1,0:T(8,128)(2,1)} %param.6) | copy-start | bytes 786436
  7.2 9.1 %slice-start.1 = ((bf16[1,128,1024]{2,1,0:T(8,128)(2,1)}), bf16[1,64,1024]{2,1,0:T(8,128)(2,1)S(1)}, s32[]{:S(2)}) async-start(bf16[1,128,1024]{2,1,0:T(8,128)(2,1)} %param.7), calls=%async_computation.4 | async-start | bytes 262144 | tf_op jit(solution)/shard_map/slice | solution.py:119
  7.2 9.1 %slice-start.3 = ((bf16[1,128,1024]{2,1,0:T(8,128)(2,1)}), bf16[1,64,1024]{2,1,0:T(8,128)(2,1)S(1)}, s32[]{:S(2)}) async-start(bf16[1,128,1024]{2,1,0:T(8,128)(2,1)} %param.5), calls=%async_computation.6 | async-start | bytes 262144 | tf_op jit(solution)/shard_map/slice | solution.py:117
  7.2 9.1 %slice-start.2 = ((bf16[1,128,1024]{2,1,0:T(8,128)(2,1)}), bf16[1,64,1024]{2,1,0:T(8,128)(2,1)S(1)}, s32[]{:S(2)}) async-start(bf16[1,128,1024]{2,1,0:T(8,128)(2,1)} %param.8), calls=%async_computation.5 | async-start | bytes 262144 | tf_op jit(solution)/shard_map/slice | solution.py:120
  7.2 51.5 %all-reduce.10.cloned.1.call-start = ((), (), s32[]{:S(2)}) async-start(), calls=%async_computation | async-start | bytes 1048576 | tf_op jit(solution)/shard_map/psum | solution.py:19
  8.3 9.2 %copy-start.5 = (bf16[1,128,1024]{2,1,0:T(8,128)(2,1)S(1)}, bf16[1,128,1024]{2,1,0:T(8,128)(2,1)}, u32[]{:S(2)}) copy-start(bf16[1,128,1024]{2,1,0:T(8,128)(2,1)} %param.7) | copy-start | bytes 786436
  9.4 19.4 %collective-permute-start.1 = (bf16[2,128,1024]{2,1,0:T(8,128)(2,1)S(1)}, bf16[2,128,1024]{2,1,0:T(8,128)(2,1)S(1)}, u32[]{:S(2)}, u32[]{:S(2)}) collective-permute-start(bf16[2,128,1024]{2,1,0:T(8,128)(2,1)S(1)} %constant_dynamic-update-slice_fusion), channel_id=1, source_target_pairs={{4,0},{8,4},{12,8},{5,1},{9,5},{13,9},{6,2},{10,6},{14,10},{7,3},{... | collective-permute-start | bytes 1572872 | tf_op jit(solution)/shard_map/ppermute | solution.py:30
  10.7 21.9 %collective-permute-start = (bf16[2,128,1024]{2,1,0:T(8,128)(2,1)S(1)}, bf16[2,128,1024]{2,1,0:T(8,128)(2,1)S(1)}, u32[]{:S(2)}, u32[]{:S(2)}) collective-permute-start(bf16[2,128,1024]{2,1,0:T(8,128)(2,1)S(1)} %constant_dynamic-update-slice_fusion), channel_id=1, source_target_pairs={{0,4},{4,8},{8,12},{1,5},{5,9},{9,13},{2,6},{6,10},{10,14},{3,7},{... | collective-permute-start | bytes 1572872 | tf_op jit(solution)/shard_map/ppermute | solution.py:27
  16.3 2.1 copy-start.14
  16.3 5.0 %copy-start.15 = (bf16[1,128,1024]{2,1,0:T(8,128)(2,1)S(1)}, bf16[1,128,1024]{2,1,0:T(8,128)(2,1)}, u32[]{:S(2)}) copy-start(bf16[1,128,1024]{2,1,0:T(8,128)(2,1)} %param.5) | copy-start | bytes 786436
  17.3 140.5 %all-reduce.12.cloned.1.call-start = ((), (), s32[]{:S(2)}) async-start(), calls=%async_computation.1 | async-start | bytes 524288 | tf_op jit(solution)/shard_map/psum | solution.py:178
  25.1 93.3 %copy-start.35 = (pred[128]{0:T(512)(128)(4,1)}, pred[128]{0:T(512)(128)(4,1)S(1)}, u32[]{:S(2)}) copy-start(pred[128]{0:T(512)(128)(4,1)S(1)} %compare_or_fusion) | copy-start | bytes 388
  63.6 1.6 copy-start.19
  66.1 1.3 copy-start.28
  66.5 2.6 %copy-start.27 = (bf16[128,256]{0,1:T(8,128)(2,1)S(1)}, bf16[128,256]{0,1:T(8,128)(2,1)}, u32[]{:S(2)}) copy-start(bf16[128,256]{0,1:T(8,128)(2,1)} %copy.108) | copy-start | bytes 196612
  66.5 2.6 %copy-start.33 = (pred[128,448]{0,1:T(8,128)(4,1)S(1)}, pred[128,448]{0,1:T(8,128)(4,1)}, u32[]{:S(2)}) copy-start(pred[128,448]{0,1:T(8,128)(4,1)} %concatenate.26) | copy-start | bytes 172036
  69.1 2.8 %copy-start.18 = (bf16[128,256]{0,1:T(8,128)(2,1)S(1)}, bf16[128,256]{0,1:T(8,128)(2,1)}, u32[]{:S(2)}) copy-start(bf16[128,256]{0,1:T(8,128)(2,1)} %copy.116) | copy-start | bytes 196612
  70.6 2.2 %copy-start.12 = (f32[4,128,448]{1,2,0:T(8,128)S(1)}, f32[4,128,448]{1,2,0:T(8,128)}, u32[]{:S(2)}) copy-start(f32[4,128,448]{1,2,0:T(8,128)} %get-tuple-element.37) | copy-start | bytes 2752516
  73.2 2.7 %copy-start.26 = (bf16[128,256]{0,1:T(8,128)(2,1)S(1)}, bf16[128,256]{0,1:T(8,128)(2,1)}, u32[]{:S(2)}) copy-start(bf16[128,256]{0,1:T(8,128)(2,1)} %copy.102) | copy-start | bytes 196612
  73.2 2.7 %copy-start.34 = (pred[128,448]{0,1:T(8,128)(4,1)S(1)}, pred[128,448]{0,1:T(8,128)(4,1)}, u32[]{:S(2)}) copy-start(pred[128,448]{0,1:T(8,128)(4,1)} %concatenate.26) | copy-start | bytes 172036
  75.9 2.8 %copy-start.17 = (bf16[128,256]{0,1:T(8,128)(2,1)S(1)}, bf16[128,256]{0,1:T(8,128)(2,1)}, u32[]{:S(2)}) copy-start(bf16[128,256]{0,1:T(8,128)(2,1)} %copy.114) | copy-start | bytes 196612
  77.3 2.2 %copy-start.13 = (f32[4,128,448]{1,2,0:T(8,128)S(1)}, f32[4,128,448]{1,2,0:T(8,128)}, u32[]{:S(2)}) copy-start(f32[4,128,448]{1,2,0:T(8,128)} %get-tuple-element.41) | copy-start | bytes 2752516
  82.4 2.4 %copy-start.7 = (bf16[448,256]{0,1:T(8,128)(2,1)}, bf16[448,256]{0,1:T(8,128)(2,1)S(1)}, u32[]{:S(2)}) copy-start(bf16[448,256]{0,1:T(8,128)(2,1)S(1)} %copy.98) | copy-start | bytes 688132
  82.4 0.9 copy-start.25
  83.3 2.8 %copy-start.16 = (bf16[128,256]{0,1:T(8,128)(2,1)S(1)}, bf16[128,256]{0,1:T(8,128)(2,1)}, u32[]{:S(2)}) copy-start(bf16[128,256]{0,1:T(8,128)(2,1)} %copy.113) | copy-start | bytes 196612
  84.8 3.3 %copy-start.11 = (f32[4,128,448]{1,2,0:T(8,128)S(1)}, f32[4,128,448]{1,2,0:T(8,128)}, u32[]{:S(2)}) copy-start(f32[4,128,448]{1,2,0:T(8,128)} %get-tuple-element.43) | copy-start | bytes 2752516
  88.5 0.8 copy-start.2
  91.1 2.5 %copy-start.1 = (f32[4,448,64]{1,2,0:T(8,128)S(1)}, f32[4,448,64]{1,2,0:T(8,128)}, u32[]{:S(2)}) copy-start(f32[4,448,64]{1,2,0:T(8,128)} %fusion.60) | copy-start | bytes 1376260
  96.2 1.5 copy-start.24
  118.7 3.8 %copy-start = (bf16[448,1024]{1,0:T(8,128)(2,1)S(1)}, bf16[448,1024]{1,0:T(8,128)(2,1)}, u32[]{:S(2)}) copy-start(bf16[448,1024]{1,0:T(8,128)(2,1)} %fusion.124) | copy-start | bytes 2752516
  121.7 2.4 %copy-start.23 = (bf16[1,64,1024]{2,1,0:T(8,128)(2,1)S(1)}, bf16[1,64,1024]{2,1,0:T(8,128)(2,1)}, u32[]{:S(2)}) copy-start(bf16[1,64,1024]{2,1,0:T(8,128)(2,1)} %get-tuple-element.23) | copy-start | bytes 393220
  121.7 91.0 %all-reduce.14.cloned.1.call-start = ((), (), s32[]{:S(2)}) async-start(), calls=%async_computation.2 | async-start | bytes 1572864 | tf_op jit(solution)/shard_map/psum | solution.py:205
  122.5 10.1 %copy-start.36 = (pred[128]{0:T(512)(128)(4,1)S(1)}, pred[128]{0:T(512)(128)(4,1)}, u32[]{:S(2)}) copy-start(pred[128]{0:T(512)(128)(4,1)} %copy-done.35) | copy-start | bytes 388
  126.3 33.0 %copy-start.37 = (pred[128]{0:T(512)(128)(4,1)S(1)}, pred[128]{0:T(512)(128)(4,1)}, u32[]{:S(2)}) copy-start(pred[128]{0:T(512)(128)(4,1)} %copy-done.35) | copy-start | bytes 388
  128.0 40.9 %collective-permute-start.3 = (bf16[2,128,1024]{2,1,0:T(8,128)(2,1)}, bf16[2,128,1024]{2,1,0:T(8,128)(2,1)}, u32[]{:S(2)}, u32[]{:S(2)}) collective-permute-start(bf16[2,128,1024]{2,1,0:T(8,128)(2,1)} %pad_maximum_fusion.4), channel_id=1, source_target_pairs={{0,4},{4,8},{8,12},{1,5},{5,9},{9,13},{2,6},{6,10},{10,14},{3,7},{... | collective-permute-start | bytes 1572872 | tf_op jit(solution)/shard_map/ppermute | solution.py:38
  159.8 1.5 copy-start.9
  159.8 1.5 copy-start.10
  160.1 3.6 %copy-start.3 = (bf16[4,128,448]{1,2,0:T(8,128)(2,1)S(1)}, bf16[4,128,448]{1,2,0:T(8,128)(2,1)}, u32[]{:S(2)}) copy-start(bf16[4,128,448]{1,2,0:T(8,128)(2,1)} %copy-done.2) | copy-start | bytes 1376260
  160.1 3.6 %copy-start.8 = (bf16[448,256]{0,1:T(8,128)(2,1)S(1)}, bf16[448,256]{0,1:T(8,128)(2,1)}, u32[]{:S(2)}) copy-start(bf16[448,256]{0,1:T(8,128)(2,1)} %copy-done.7) | copy-start | bytes 688132
  162.2 2.9 %copy-start.20 = (f32[4,64,128]{2,1,0:T(8,128)S(1)}, f32[4,64,128]{2,1,0:T(8,128)}, u32[]{:S(2)}) copy-start(f32[4,64,128]{2,1,0:T(8,128)} %convolution_multiply_fusion.12) | copy-start | bytes 393220
  162.2 3.1 %copy-start.29 = (bf16[4,64,128]{2,1,0:T(8,128)(2,1)S(1)}, bf16[4,64,128]{2,1,0:T(8,128)(2,1)}, u32[]{:S(2)}) copy-start(bf16[4,64,128]{2,1,0:T(8,128)(2,1)} %get-tuple-element.49) | copy-start | bytes 196612
  162.2 3.2 %copy-start.21 = (f32[4,64,128]{2,1,0:T(8,128)S(1)}, f32[4,64,128]{2,1,0:T(8,128)}, u32[]{:S(2)}) copy-start(f32[4,64,128]{2,1,0:T(8,128)} %convolution_multiply_fusion.11) | copy-start | bytes 393220
  162.2 3.3 %copy-start.30 = (bf16[4,64,128]{2,1,0:T(8,128)(2,1)S(1)}, bf16[4,64,128]{2,1,0:T(8,128)(2,1)}, u32[]{:S(2)}) copy-start(bf16[4,64,128]{2,1,0:T(8,128)(2,1)} %get-tuple-element.47) | copy-start | bytes 196612
  162.2 27.4 %collective-permute-start.2 = (bf16[2,128,1024]{2,1,0:T(8,128)(2,1)}, bf16[2,128,1024]{2,1,0:T(8,128)(2,1)}, u32[]{:S(2)}, u32[]{:S(2)}) collective-permute-start(bf16[2,128,1024]{2,1,0:T(8,128)(2,1)} %pad_maximum_fusion.3), channel_id=1, source_target_pairs={{4,0},{8,4},{12,8},{5,1},{9,5},{13,9},{6,2},{10,6},{14,10},{7,3},{... | collective-permute-start | bytes 1572872 | tf_op jit(solution)/shard_map/ppermute | solution.py:38
  164.5 2.1 copy-start.31
  164.5 2.2 copy-start.22
  164.5 3.0 %copy-start.32 = (bf16[4,64,128]{2,1,0:T(8,128)(2,1)S(1)}, bf16[4,64,128]{2,1,0:T(8,128)(2,1)}, u32[]{:S(2)}) copy-start(bf16[4,64,128]{2,1,0:T(8,128)(2,1)} %get-tuple-element.53) | copy-start | bytes 196612
  165.1 2.9 %copy-start.6 = (f32[64,1024]{1,0:T(8,128)S(1)}, f32[64,1024]{1,0:T(8,128)}, u32[]{:S(2)}) copy-start(f32[64,1024]{1,0:T(8,128)} %all-reduce.12.cloned.1.call-done) | copy-start | bytes 786436
  165.5 2.6 %copy-start.38 = (pred[128]{0:T(512)(128)(4,1)S(1)}, pred[128]{0:T(512)(128)(4,1)}, u32[]{:S(2)}) copy-start(pred[128]{0:T(512)(128)(4,1)} %broadcast_compare_fusion.1) | copy-start | bytes 388
Sparse Core Ops, SparseCore 0:
  17.4 41.3 all-reduce.9
  121.8 35.8 all-reduce.11
  161.4 51.2 all-reduce.13
where the time goes:
time: 223 us; the launch traced here: 222 us
  waiting for transfers between devices  99.2 us (44%)
  local copies, waits for them, and re-layouts  33.2 us (15%)
  matrix products  22.1 us (10%)
  blocking collectives  19.7 us (9%)
  other arithmetic  19.3 us (9%)
  between operations  15.4 us (7%)
  starting transfers between devices  13 us (6%)
    psum x1, waiting for transfers between devices, broadcast(): return lax.psum(block, axis)  26 us
    psum x1, waiting for transfers between devices, per_device(): weight_sums, weighted = lax.psum((weight_sums, weighted), 'seq')  24.8 us
    psum x1, waiting for transfers between devices, per_device(): lax.psum((suffix_terms[0], suffix_terms[1], suffix_terms[2]), 'seq')  22 us
    ppermute x2, waiting for transfers between devices, shifted(): return lax.ppermute(block, axis, route)  19.5 us
    pmax x1, blocking collectives, per_device(): glob_top = lax.pmax(jnp.max(gscores, axis=2), 'seq')  11 us
    reshape x18, local copies, waits for them, and re-layouts, join_heads(): return block_rows.reshape(block_rows.shape[0], -1)  9.07 us
    psum x1, blocking collectives, per_device(): weight_sums, weighted = lax.psum((weight_sums, weighted), 'seq')  8.7 us
    ppermute x2, starting transfers between devices, shifted(): return lax.ppermute(block, axis, route)  6.04 us
  transfers between devices with their start and end apart: 7, of which 6 were waited for; matrix products, arithmetic and copies ran while one was open for 12% of the time, Pallas kernels for 0%

commit v1 on v0

v1 whole, which is shorter than its diff:
```python
import functools
import math

import jax
import jax.numpy as jnp
from jax import lax
from jax.experimental import pallas as pl
from jax.experimental.pallas import tpu as pltpu
from jax.sharding import PartitionSpec as P

D = 1024
H = 16
W = 128
G = 64
HEAD = D // H
PAIR = 2 * HEAD

MESH = pl.DeviceIdType.MESH
very_negative = -1e30
scale = 1.0 / math.sqrt(HEAD)
f32 = jnp.float32
bf16 = jnp.bfloat16


def dot_nt(a, b):
    return lax.dot_general(a, b, (((1,), (1,)), ((), ())), preferred_element_type=f32)


def dot_nn(a, b):
    return lax.dot_general(a, b, (((1,), (0,)), ((), ())), preferred_element_type=f32)


def dot_tn(a, b):
    return lax.dot_general(a, b, (((0,), (0,)), ((), ())), preferred_element_type=f32)


def iota(shape, dim):
    return lax.broadcasted_iota(jnp.int32, shape, dim)


def pair_mask(value):
    lane = iota((1, PAIR), 1)
    first = jnp.where(lane < HEAD, value, 0.0).astype(bf16)
    second = jnp.where(lane < HEAD, 0.0, value).astype(bf16)
    return first, second


def two_heads(rows, value):
    first, second = pair_mask(value)
    return jnp.concatenate([rows * first, rows * second], axis=0)


def one_pair(stacked):
    half = stacked.shape[0] // 2
    lane = iota((half, PAIR), 1)
    return jnp.where(lane < HEAD, stacked[:half], stacked[half:])


def kernel(
    n, rows, chunks,
    pad_ref, q_ref, k_ref, v_ref, g_ref,
    att_ref, qgrad_ref, kgrad_ref, vgrad_ref,
    kv, qg, stats, bias, key_bias, expo_s, dprob_s,
    own_grad, suf_grad, down_out, down_in, up_out, up_in, chain_out, chain_in,
    qg_send, qg_recv, suf_send, suf_recv, low_send, low_recv, high_send, high_recv,
    stat_send, stat_recv, down_send, down_recv, up_send, up_recv, chain_send, chain_recv,
):
    me = lax.axis_index("seq")
    last = n - 1
    below = lax.rem(me + n - 1, n)
    above = lax.rem(me + 1, n)
    has_below = me > 0
    has_above = me < last
    all_keys = rows + 2 * W + G
    own = slice(W, W + rows)
    low = slice(0, W)
    high = slice(W + rows, 2 * W + rows)
    suf = slice(2 * W + rows, all_keys)
    tail = slice(rows - G, rows)

    def remote(src, dst, send, recv, target):
        return pltpu.make_async_remote_copy(
            src_ref=src, dst_ref=dst, send_sem=send, recv_sem=recv,
            device_id={"seq": target}, device_id_type=MESH,
        )

    def send_qg(c):
        return remote(qg.at[c], qg.at[c], qg_send.at[c], qg_recv.at[c], below)

    def send_suf(c):
        return remote(kv.at[c, :, suf], kv.at[c, :, suf], suf_send.at[c], suf_recv.at[c], below)

    def send_low(c):
        return remote(kv.at[c, :, own], kv.at[c, :, high], low_send.at[c], low_recv.at[c], below)

    def send_high(c):
        return remote(kv.at[c, :, own], kv.at[c, :, low], high_send.at[c], high_recv.at[c], above)

    def send_down(c):
        return remote(down_out.at[c], down_in.at[c], down_send.at[c], down_recv.at[c], below)

    def send_up(c):
        return remote(up_out.at[c], up_in.at[c], up_send.at[c], up_recv.at[c], above)

    def send_chain(c):
        return remote(chain_out.at[c], chain_in.at[c], chain_send.at[c], chain_recv.at[c], above)

    def send_stats(k):
        return remote(
            stats.at[0], stats.at[k], stat_send.at[k], stat_recv.at[k], lax.rem(me + k, n)
        )

    barrier = pltpu.get_barrier_semaphore()
    for k in range(1, n):
        pl.semaphore_signal(
            barrier, inc=1, device_id={"seq": lax.rem(me + k, n)}, device_id_type=MESH
        )

    for c in range(chunks):
        columns = slice(c * PAIR, (c + 1) * PAIR)
        kv[c, 0, own] = k_ref[:, columns]
        kv[c, 1, own] = v_ref[:, columns]

    @pl.when(me == last)
    def _():
        for c in range(chunks):
            columns = slice(c * PAIR, (c + 1) * PAIR)
            qg[c, 0] = q_ref[tail, columns]
            qg[c, 1] = g_ref[tail, columns]
            kv[c, 0, suf] = k_ref[tail, columns]
            kv[c, 1, suf] = v_ref[tail, columns]
            kv[c, :, high] = jnp.zeros((2, W, PAIR), bf16)

    @pl.when(me == 0)
    def _():
        for c in range(chunks):
            kv[c, :, low] = jnp.zeros((2, W, PAIR), bf16)

    pl.semaphore_wait(barrier, n - 1)

    @pl.when(has_above)
    def _():
        for c in range(chunks):
            send_high(c).start()

    @pl.when(me == last)
    def _():
        for c in range(chunks):
            send_qg(c).start()
        for c in range(chunks):
            send_suf(c).start()
            send_low(c).start()

    suffix_start = rows * n - G
    valid_end = suffix_start - pad_ref[0]
    first_row = me * rows
    j = iota((all_keys, 2 * rows), 0)
    i = iota((all_keys, 2 * rows), 1)
    i = jnp.where(i >= rows, i - rows, i)
    key_pos = first_row - W + j
    apart = i - (j - W)
    within = (apart <= W) & (apart >= -W) & (key_pos >= 0) & (key_pos < valid_end)
    bias[...] = jnp.where(within | (j >= 2 * W + rows), 0.0, very_negative)
    own_pos = first_row + iota((rows, 2 * G), 0)
    key_bias[...] = jnp.where(
        (own_pos < valid_end) | (own_pos >= suffix_start), 0.0, very_negative
    )
    query_lane = iota((1, 2 * rows), 1)
    query_pos = first_row + jnp.where(query_lane >= rows, query_lane - rows, query_lane)
    row_live = jnp.where(query_pos < suffix_start, 1.0, 0.0)

    def forward_stats(c, carry):
        @pl.when(has_above)
        def _():
            send_qg(c).wait_recv()

            @pl.when(has_below)
            def _():
                send_qg(c).start()

        query_two = two_heads(qg[c, 0], scale)
        grad_two = two_heads(qg[c, 1], 1.0)
        scores = dot_nt(kv[c, 0, own], query_two) + key_bias[...]
        largest = jnp.max(scores, axis=0, keepdims=True)
        expo = jnp.exp(scores - largest)
        dprob = dot_nt(kv[c, 1, own], grad_two)
        total = jnp.sum(expo, axis=0, keepdims=True)
        weighted = jnp.sum(expo * dprob, axis=0, keepdims=True)
        expo_s[c] = expo
        dprob_s[c] = dprob
        row = iota((8, 2 * G), 0)
        stats[0, c] = jnp.where(row == 0, largest, jnp.where(row == 1, total, weighted))
        return carry

    lax.fori_loop(0, chunks, forward_stats, 0)
    for k in range(1, n):
        send_stats(k).start()

    def band(c, carry):
        @pl.when(has_above)
        def _():
            send_suf(c).wait_recv()

            @pl.when(has_below)
            def _():
                send_suf(c).start()
                send_low(c).start()

        @pl.when(has_below)
        def _():
            send_high(c).wait_recv()

        @pl.when(has_above)
        def _():
            send_low(c).wait_recv()

        columns = pl.ds(pl.multiple_of(c * PAIR, PAIR), PAIR)
        query_two = two_heads(q_ref[:, columns], scale)
        grad_two = two_heads(g_ref[:, columns], 1.0)
        keys = kv[c, 0]
        values = kv[c, 1]
        scores = dot_nt(keys, query_two) + bias[...]
        largest = jnp.max(scores, axis=0, keepdims=True)
        expo = jnp.exp(scores - largest)
        total = jnp.sum(expo, axis=0, keepdims=True)
        dprob = dot_nt(values, grad_two)
        inverse = 1.0 / total
        delta = jnp.sum(expo * dprob, axis=0, keepdims=True) * inverse
        probs = expo * (inverse * row_live)
        probs_low = probs.astype(bf16)
        dscore = (probs * (dprob - delta)).astype(bf16)
        att_ref[:, columns] = one_pair(dot_tn(probs_low, values)).astype(bf16)
        qgrad_ref[:, columns] = (one_pair(dot_tn(dscore, keys)) * scale).astype(bf16)
        key_all = dot_nn(dscore, query_two)
        value_all = dot_nn(probs_low, grad_two)
        down_out[c, 0] = key_all[low].astype(bf16)
        down_out[c, 1] = value_all[low].astype(bf16)
        up_out[c, 0] = key_all[high].astype(bf16)
        up_out[c, 1] = value_all[high].astype(bf16)

        @pl.when(has_below)
        def _():
            send_down(c).start()

        @pl.when(has_above)
        def _():
            send_up(c).start()

        own_grad[c, 0] = key_all[own]
        own_grad[c, 1] = value_all[own]
        suf_grad[c, 0] = key_all[suf]
        suf_grad[c, 1] = value_all[suf]
        return carry


    lax.fori_loop(0, chunks, band, 0)

    for k in range(1, n):
        send_stats(k).wait_recv()

    def finish(c, carry):
        columns = pl.ds(pl.multiple_of(c * PAIR, PAIR), PAIR)
        parts = [stats[k, c] for k in range(n)]
        top = parts[0][0:1]
        for part in parts[1:]:
            top = jnp.maximum(top, part[0:1])
        factors = [jnp.exp(part[0:1] - top) for part in parts]
        total = sum(factor * part[1:2] for factor, part in zip(factors, parts))
        weighted = sum(factor * part[2:3] for factor, part in zip(factors, parts))
        inverse = 1.0 / total
        delta = weighted * inverse
        probs = expo_s[c] * (factors[0] * inverse)
        probs_low = probs.astype(bf16)
        dscore = (probs * (dprob_s[c] - delta)).astype(bf16)
        query_two = two_heads(qg[c, 0], scale)
        grad_two = two_heads(qg[c, 1], 1.0)
        att_part = one_pair(dot_tn(probs_low, kv[c, 1, own]))
        query_part = one_pair(dot_tn(dscore, kv[c, 0, own])) * scale
        suf_key = suf_grad[c, 0]
        suf_value = suf_grad[c, 1]
        key_sum = own_grad[c, 0] + dot_nn(dscore, query_two)
        value_sum = own_grad[c, 1] + dot_nn(probs_low, grad_two)

        @pl.when(me == 0)
        def _():
            chain_out[c, 0] = att_part.astype(bf16)
            chain_out[c, 1] = query_part.astype(bf16)
            chain_out[c, 2] = suf_key.astype(bf16)
            chain_out[c, 3] = suf_value.astype(bf16)

        own_grad[c, 0] = key_sum
        own_grad[c, 1] = value_sum

        @pl.when(has_below)
        def _():
            send_chain(c).wait_recv()
            att_sum = att_part + chain_in[c, 0].astype(f32)
            query_sum = query_part + chain_in[c, 1].astype(f32)
            key_suf = suf_key + chain_in[c, 2].astype(f32)
            value_suf = suf_value + chain_in[c, 3].astype(f32)

            @pl.when(has_above)
            def _():
                chain_out[c, 0] = att_sum.astype(bf16)
                chain_out[c, 1] = query_sum.astype(bf16)
                chain_out[c, 2] = key_suf.astype(bf16)
                chain_out[c, 3] = value_suf.astype(bf16)

            @pl.when(me == last)
            def _():
                att_ref[tail, columns] = att_sum.astype(bf16)
                qgrad_ref[tail, columns] = query_sum.astype(bf16)
                own_grad[c, 0, tail] = own_grad[c, 0, tail] + key_suf
                own_grad[c, 1, tail] = own_grad[c, 1, tail] + value_suf

        @pl.when(has_above)
        def _():
            send_chain(c).start()

        return carry

    lax.fori_loop(0, chunks, finish, 0)

    def combine(c, carry):
        columns = pl.ds(pl.multiple_of(c * PAIR, PAIR), PAIR)

        @pl.when(has_below)
        def _():
            send_up(c).wait_recv()
            own_grad[c, :, 0:W] = own_grad[c, :, 0:W] + up_in[c].astype(f32)

        @pl.when(has_above)
        def _():
            send_down(c).wait_recv()
            own_grad[c, :, rows - W : rows] = own_grad[c, :, rows - W : rows] + down_in[
                c
            ].astype(f32)

        kgrad_ref[:, columns] = own_grad[c, 0].astype(bf16)
        vgrad_ref[:, columns] = own_grad[c, 1].astype(bf16)
        return carry

    lax.fori_loop(0, chunks, combine, 0)

    def drain(c, carry):
        @pl.when(has_below)
        def _():
            send_qg(c).wait_send()
            send_suf(c).wait_send()
            send_low(c).wait_send()
            send_down(c).wait_send()

        @pl.when(has_above)
        def _():
            send_high(c).wait_send()
            send_up(c).wait_send()
            send_chain(c).wait_send()

        return carry

    lax.fori_loop(0, chunks, drain, 0)
    for k in range(1, n):
        send_stats(k).wait_send()


def per_device(n, query_vectors, key_vectors, value_vectors, out_grad, pad_length):
    rows, features = query_vectors.shape[1:]
    chunks = features // PAIR
    all_keys = rows + 2 * W + G
    vmem = pl.BlockSpec(memory_space=pltpu.VMEM)
    smem = pl.BlockSpec(memory_space=pltpu.SMEM)
    out = jax.ShapeDtypeStruct((rows, features), bf16)
    dma = pltpu.SemaphoreType.DMA
    outs = pl.pallas_call(
        functools.partial(kernel, n, rows, chunks),
        out_shape=(out,) * 4,
        in_specs=[smem] + [vmem] * 4,
        out_specs=(vmem,) * 4,
        scratch_shapes=[
            pltpu.VMEM((chunks, 2, all_keys, PAIR), bf16),
            pltpu.VMEM((chunks, 2, G, PAIR), bf16),
            pltpu.VMEM((n, chunks, 8, 2 * G), f32),
            pltpu.VMEM((all_keys, 2 * rows), f32),
            pltpu.VMEM((rows, 2 * G), f32),
            pltpu.VMEM((chunks, rows, 2 * G), f32),
            pltpu.VMEM((chunks, rows, 2 * G), f32),
            pltpu.VMEM((chunks, 2, rows, PAIR), f32),
            pltpu.VMEM((chunks, 2, G, PAIR), f32),
            pltpu.VMEM((chunks, 2, W, PAIR), bf16),
            pltpu.VMEM((chunks, 2, W, PAIR), bf16),
            pltpu.VMEM((chunks, 2, W, PAIR), bf16),
            pltpu.VMEM((chunks, 2, W, PAIR), bf16),
            pltpu.VMEM((chunks, 4, G, PAIR), bf16),
            pltpu.VMEM((chunks, 4, G, PAIR), bf16),
        ]
        + [dma((chunks,))] * 8
        + [dma((n,))] * 2
        + [dma((chunks,))] * 6,
        compiler_params=pltpu.CompilerParams(
            collective_id=0, has_side_effects=True, vmem_limit_bytes=48 << 20
        ),
    )(pad_length, query_vectors[0], key_vectors[0], value_vectors[0], out_grad[0])
    return tuple(array[None] for array in outs)


def solution(mesh):
    rows = P(("group", "doc"), "seq", None)
    return jax.shard_map(
        functools.partial(per_device, mesh.shape["seq"]),
        mesh=mesh,
        in_specs=(rows, rows, rows, rows, P(("group", "doc"))),
        out_specs=(rows,) * 4,
        check_vma=False,
    )
```

time: 223 us -> 74.3 us (0.33)
  the two profiles are of different devices: /device:TPU:0 before, /device:TPU:28 now
where the time goes in v1:
time: 74.3 us; the launch traced here: 74 us
  Pallas kernels  66.1 us (89%)
  local copies, waits for them, and re-layouts  6.6 us (9%)
  between operations  1.3 us (2%)
    pallas_call x1, Pallas kernels, per_device(): pl.pallas_call(functools.partial(kernel, n, rows, chunks), out_shape=(out...  66.1 us
    unnamed x12, local copies, waits for them, and re-layouts  6.6 us

profile of v1, /device:TPU:28, one launch (start us, length us, event | category | flops | bytes accessed | tf_op | source)
XLA Modules:
  0.0 74.0 jit_solution(11514810587512738584)
XLA Ops:
  1.3 0.0 copy-start
  1.3 0.9 %copy-done = bf16[1,128,1024]{2,1,0:T(8,128)(2,1)S(1)} copy-done((bf16[1,128,1024]{2,1,0:T(8,128)(2,1)S(1)}, bf16[1,128,1024]{2,1,0:T(8,128)(2,1)}, u32[]{:S(2)}) %copy-start) | copy-done | bytes 262168
  2.2 0.0 copy-start.1
  2.2 0.9 %copy-done.1 = bf16[1,128,1024]{2,1,0:T(8,128)(2,1)S(1)} copy-done((bf16[1,128,1024]{2,1,0:T(8,128)(2,1)S(1)}, bf16[1,128,1024]{2,1,0:T(8,128)(2,1)}, u32[]{:S(2)}) %copy-start.1) | copy-done | bytes 262168
  3.2 0.0 copy-start.2
  3.2 0.9 %copy-done.2 = bf16[1,128,1024]{2,1,0:T(8,128)(2,1)S(1)} copy-done((bf16[1,128,1024]{2,1,0:T(8,128)(2,1)S(1)}, bf16[1,128,1024]{2,1,0:T(8,128)(2,1)}, u32[]{:S(2)}) %copy-start.2) | copy-done | bytes 262168
  4.1 0.0 copy-start.3
  4.1 0.9 %copy-done.3 = bf16[1,128,1024]{2,1,0:T(8,128)(2,1)S(1)} copy-done((bf16[1,128,1024]{2,1,0:T(8,128)(2,1)S(1)}, bf16[1,128,1024]{2,1,0:T(8,128)(2,1)}, u32[]{:S(2)}) %copy-start.3) | copy-done | bytes 262168
  5.1 66.1 %shard_map.84 = (bf16[128,1024]{1,0:T(8,128)(2,1)S(1)}, bf16[128,1024]{1,0:T(8,128)(2,1)S(1)}, bf16[128,1024]{1,0:T(8,128)(2,1)S(1)}, bf16[128,1024]{1,0:T(8,128)(2,1)S(1)}) custom-call(s32[1]{0:T(128)S(6)} %copy.13.pad_ref, bf16[128,1024]{1,0:T(8,128)(2,1)S(1)} %bitcast.12, bf16[128,1024]{1,0:T(8,128)(2,1)S(1)} %bitcast.13, bf16[128,1024]{1,0:T(8,128)(2,1)S(1)} %bitcast.14, ...), custom_call_target="tpu_custom_call" | custom-call | tf_op jit(solution)/shard_map/pallas_call | solution.py:374
  71.2 0.7 copy.14
  71.9 0.7 copy.15
  72.6 0.7 copy.16
  73.3 0.7 copy.17
Async XLA Ops:
  1.3 1.0 %copy-start = (bf16[1,128,1024]{2,1,0:T(8,128)(2,1)S(1)}, bf16[1,128,1024]{2,1,0:T(8,128)(2,1)}, u32[]{:S(2)}) copy-start(bf16[1,128,1024]{2,1,0:T(8,128)(2,1)} %param.5) | copy-start | bytes 786436
  2.2 0.9 %copy-start.1 = (bf16[1,128,1024]{2,1,0:T(8,128)(2,1)S(1)}, bf16[1,128,1024]{2,1,0:T(8,128)(2,1)}, u32[]{:S(2)}) copy-start(bf16[1,128,1024]{2,1,0:T(8,128)(2,1)} %param.6) | copy-start | bytes 786436
  3.2 0.9 %copy-start.2 = (bf16[1,128,1024]{2,1,0:T(8,128)(2,1)S(1)}, bf16[1,128,1024]{2,1,0:T(8,128)(2,1)}, u32[]{:S(2)}) copy-start(bf16[1,128,1024]{2,1,0:T(8,128)(2,1)} %param.7) | copy-start | bytes 786436
  4.1 0.9 %copy-start.3 = (bf16[1,128,1024]{2,1,0:T(8,128)(2,1)S(1)}, bf16[1,128,1024]{2,1,0:T(8,128)(2,1)}, u32[]{:S(2)}) copy-start(bf16[1,128,1024]{2,1,0:T(8,128)(2,1)} %param.8) | copy-start | bytes 786436

commit v2 on v1

--- a/solution.py
+++ b/solution.py
@@ -14,6 +14,10 @@
 G = 64
 HEAD = D // H
 PAIR = 2 * HEAD
+AHEAD = 2
+CHAIN_LAG = 3
+UP_LAG = 2
+DOWN_LAG = 2
 
 MESH = pl.DeviceIdType.MESH
 very_negative = -1e30
@@ -60,9 +64,9 @@
     n, rows, chunks,
     pad_ref, q_ref, k_ref, v_ref, g_ref,
     att_ref, qgrad_ref, kgrad_ref, vgrad_ref,
-    kv, qg, stats, bias, key_bias, expo_s, dprob_s,
+    kv, qg, own_qg, stats, bias, key_bias, expo_s, dprob_s,
     own_grad, suf_grad, down_out, down_in, up_out, up_in, chain_out, chain_in,
-    qg_send, qg_recv, suf_send, suf_recv, low_send, low_recv, high_send, high_recv,
+    load_sem, qg_send, qg_recv, suf_send, suf_recv, low_send, low_recv, high_send, high_recv,
     stat_send, stat_recv, down_send, down_recv, up_send, up_recv, chain_send, chain_recv,
 ):
     me = lax.axis_index("seq")
@@ -77,6 +81,7 @@
     high = slice(W + rows, 2 * W + rows)
     suf = slice(2 * W + rows, all_keys)
     tail = slice(rows - G, rows)
+    near = min(W, rows - G)
 
     def remote(src, dst, send, recv, target):
         return pltpu.make_async_remote_copy(
@@ -93,6 +98,18 @@
     def send_low(c):
         return remote(kv.at[c, :, own], kv.at[c, :, high], low_send.at[c], low_recv.at[c], below)
 
+    def send_low_last(c):
+        return remote(
+            kv.at[c, :, W : W + near],
+            kv.at[c, :, W + rows : W + rows + near],
+            low_send.at[c], low_recv.at[c], below,
+        )
+
+    def send_up_last(c):
+        return remote(
+            up_out.at[c, :, :near], up_in.at[c, :, :near], up_send.at[c], up_recv.at[c], above
+        )
+
     def send_high(c):
         return remote(kv.at[c, :, own], kv.at[c, :, low], high_send.at[c], high_recv.at[c], above)
 
@@ -116,26 +133,44 @@
             barrier, inc=1, device_id={"seq": lax.rem(me + k, n)}, device_id_type=MESH
         )
 
+    loads = []
     for c in range(chunks):
-        columns = slice(c * PAIR, (c + 1) * PAIR)
-        kv[c, 0, own] = k_ref[:, columns]
-        kv[c, 1, own] = v_ref[:, columns]
+        columns = pl.ds(c * PAIR, PAIR)
+        pieces = (
+            (k_ref, kv.at[c, 0, own]),
+            (v_ref, kv.at[c, 1, own]),
+            (q_ref, own_qg.at[c, 0]),
+            (g_ref, own_qg.at[c, 1]),
+        )
+        for k, (source, target) in enumerate(pieces):
+            copy = pltpu.make_async_copy(source.at[0, :, columns], target, load_sem.at[c, k])
+            copy.start()
+            loads.append(copy)
 
     @pl.when(me == last)
     def _():
         for c in range(chunks):
-            columns = slice(c * PAIR, (c + 1) * PAIR)
-            qg[c, 0] = q_ref[tail, columns]
-            qg[c, 1] = g_ref[tail, columns]
-            kv[c, 0, suf] = k_ref[tail, columns]
-            kv[c, 1, suf] = v_ref[tail, columns]
             kv[c, :, high] = jnp.zeros((2, W, PAIR), bf16)
 
+    @pl.when(me == last - 1)
+    def _():
+        for c in range(chunks):
+            kv[c, :, W + rows + near : 2 * W + rows] = jnp.zeros((2, W - near, PAIR), bf16)
+
     @pl.when(me == 0)
     def _():
         for c in range(chunks):
             kv[c, :, low] = jnp.zeros((2, W, PAIR), bf16)
 
+    for copy in loads:
+        copy.wait()
+
+    @pl.when(me == last)
+    def _():
+        for c in range(chunks):
+            qg[c] = own_qg[c, :, tail]
+            kv[c, :, suf] = kv[c, :, W + rows - G : W + rows]
+
     pl.semaphore_wait(barrier, n - 1)
 
     @pl.when(has_above)
@@ -147,8 +182,13 @@
     def _():
         for c in range(chunks):
             send_qg(c).start()
-        for c in range(chunks):
             send_suf(c).start()
+        for c in range(chunks):
+            send_low_last(c).start()
+
+    @pl.when(has_above & has_below)
+    def _():
+        for c in range(AHEAD):
             send_low(c).start()
 
     suffix_start = rows * n - G
@@ -178,6 +218,12 @@
             def _():
                 send_qg(c).start()
 
+            send_suf(c).wait_recv()
+
+            @pl.when(has_below)
+            def _():
+                send_suf(c).start()
+
         query_two = two_heads(qg[c, 0], scale)
         grad_two = two_heads(qg[c, 1], 1.0)
         scores = dot_nt(kv[c, 0, own], query_two) + key_bias[...]
@@ -196,27 +242,27 @@
     for k in range(1, n):
         send_stats(k).start()
 
-    def band(c, carry):
-        @pl.when(has_above)
-        def _():
-            send_suf(c).wait_recv()
-
-            @pl.when(has_below)
-            def _():
-                send_suf(c).start()
-                send_low(c).start()
-
+    @pl.when(has_above & has_below)
+    def _():
+        for c in range(AHEAD, chunks):
+            send_low(c).start()
+
+    def band(c):
         @pl.when(has_below)
         def _():
             send_high(c).wait_recv()
 
-        @pl.when(has_above)
+        @pl.when(me < last - 1)
         def _():
             send_low(c).wait_recv()
 
+        @pl.when(me == last - 1)
+        def _():
+            send_low_last(c).wait_recv()
+
         columns = pl.ds(pl.multiple_of(c * PAIR, PAIR), PAIR)
-        query_two = two_heads(q_ref[:, columns], scale)
-        grad_two = two_heads(g_ref[:, columns], 1.0)
+        query_two = two_heads(own_qg[c, 0], scale)
+        grad_two = two_heads(own_qg[c, 1], 1.0)
         keys = kv[c, 0]
         values = kv[c, 1]
         scores = dot_nt(keys, query_two) + bias[...]
@@ -238,27 +284,12 @@
         up_out[c, 0] = key_all[high].astype(bf16)
         up_out[c, 1] = value_all[high].astype(bf16)
 
-        @pl.when(has_below)
-        def _():
-            send_down(c).start()
-
-        @pl.when(has_above)
-        def _():
-            send_up(c).start()
-
         own_grad[c, 0] = key_all[own]
         own_grad[c, 1] = value_all[own]
         suf_grad[c, 0] = key_all[suf]
         suf_grad[c, 1] = value_all[suf]
-        return carry
-
-
-    lax.fori_loop(0, chunks, band, 0)
-
-    for k in range(1, n):
-        send_stats(k).wait_recv()
-
-    def finish(c, carry):
+
+    def finish(c):
         columns = pl.ds(pl.multiple_of(c * PAIR, PAIR), PAIR)
         parts = [stats[k, c] for k in range(n)]
         top = parts[0][0:1]
@@ -317,17 +348,58 @@
         def _():
             send_chain(c).start()
 
+    lag = jnp.minimum(CHAIN_LAG * me, chunks)
+
+    def step(t, carry):
+        @pl.when(t < chunks)
+        def _():
+            band(t)
+
+            @pl.when(me == last)
+            def _():
+                send_low_last(t).wait_send()
+
+        @pl.when(t == lag)
+        def _():
+            for k in range(1, n):
+                send_stats(k).wait_recv()
+
+        @pl.when((t >= lag) & (t < lag + chunks))
+        def _():
+            finish(t - lag)
+
+        @pl.when((t >= UP_LAG) & (t < UP_LAG + chunks))
+        def _():
+            @pl.when(me < last - 1)
+            def _():
+                send_up(t - UP_LAG).start()
+
+            @pl.when(me == last - 1)
+            def _():
+                send_up_last(t - UP_LAG).start()
+
+        @pl.when((t >= DOWN_LAG) & (t < DOWN_LAG + chunks) & has_below)
+        def _():
+            send_down(t - DOWN_LAG).start()
+
         return carry
 
-    lax.fori_loop(0, chunks, finish, 0)
+    lax.fori_loop(0, 2 * chunks, step, 0)
 
     def combine(c, carry):
         columns = pl.ds(pl.multiple_of(c * PAIR, PAIR), PAIR)
 
         @pl.when(has_below)
         def _():
-            send_up(c).wait_recv()
-            own_grad[c, :, 0:W] = own_grad[c, :, 0:W] + up_in[c].astype(f32)
+            @pl.when(me < last)
+            def _():
+                send_up(c).wait_recv()
+                own_grad[c, :, 0:W] = own_grad[c, :, 0:W] + up_in[c].astype(f32)
+
+            @pl.when(me == last)
+            def _():
+                send_up_last(c).wait_recv()
+                own_grad[c, :, 0:near] = own_grad[c, :, 0:near] + up_in[c, :, 0:near].astype(f32)
 
         @pl.when(has_above)
         def _():
@@ -347,14 +419,25 @@
         def _():
             send_qg(c).wait_send()
             send_suf(c).wait_send()
-            send_low(c).wait_send()
+
+            @pl.when(has_above)
+            def _():
+                send_low(c).wait_send()
+
             send_down(c).wait_send()
 
         @pl.when(has_above)
         def _():
             send_high(c).wait_send()
+            send_chain(c).wait_send()
+
+        @pl.when(me < last - 1)
+        def _():
             send_up(c).wait_send()
-            send_chain(c).wait_send()
+
+        @pl.when(me == last - 1)
+        def _():
+            send_up_last(c).wait_send()
 
         return carry
 
@@ -374,11 +457,12 @@
     outs = pl.pallas_call(
         functools.partial(kernel, n, rows, chunks),
         out_shape=(out,) * 4,
-        in_specs=[smem] + [vmem] * 4,
+        in_specs=[smem] + [pl.BlockSpec(memory_space=pl.ANY)] * 4,
         out_specs=(vmem,) * 4,
         scratch_shapes=[
             pltpu.VMEM((chunks, 2, all_keys, PAIR), bf16),
             pltpu.VMEM((chunks, 2, G, PAIR), bf16),
+            pltpu.VMEM((chunks, 2, rows, PAIR), bf16),
             pltpu.VMEM((n, chunks, 8, 2 * G), f32),
             pltpu.VMEM((all_keys, 2 * rows), f32),
             pltpu.VMEM((rows, 2 * G), f32),
@@ -393,13 +477,14 @@
             pltpu.VMEM((chunks, 4, G, PAIR), bf16),
             pltpu.VMEM((chunks, 4, G, PAIR), bf16),
         ]
+        + [dma((chunks, 4))]
         + [dma((chunks,))] * 8
         + [dma((n,))] * 2
         + [dma((chunks,))] * 6,
         compiler_params=pltpu.CompilerParams(
             collective_id=0, has_side_effects=True, vmem_limit_bytes=48 << 20
         ),
-    )(pad_length, query_vectors[0], key_vectors[0], value_vectors[0], out_grad[0])
+    )(pad_length, query_vectors, key_vectors, value_vectors, out_grad)
     return tuple(array[None] for array in outs)
 
 

time: 74.3 us -> 61.2 us (0.82)
  Pallas kernels: 66.1 us -> 53 us
    pallas_call x1, Pallas kernels: 66.1 us -> 53 us  [per_device(): pl.pallas_call(functools.partial(kernel, n, rows, chunks), out_shape=(out...]
where the time goes in v2:
time: 61.2 us; the launch traced here: 60.9 us
  Pallas kernels  53 us (87%)
  local copies, waits for them, and re-layouts  6.6 us (11%)
  between operations  1.3 us (2%)
    pallas_call x1, Pallas kernels, per_device(): pl.pallas_call(functools.partial(kernel, n, rows, chunks), out_shape=(out...  53 us
    unnamed x12, local copies, waits for them, and re-layouts  6.6 us

profile of v2, /device:TPU:28, one launch (start us, length us, event | category | flops | bytes accessed | tf_op | source)
XLA Modules:
  0.0 60.9 jit_solution(637118446090789128)
XLA Ops:
  1.3 0.0 copy-start
  1.3 0.9 %copy-done = bf16[1,128,1024]{2,1,0:T(8,128)(2,1)S(1)} copy-done((bf16[1,128,1024]{2,1,0:T(8,128)(2,1)S(1)}, bf16[1,128,1024]{2,1,0:T(8,128)(2,1)}, u32[]{:S(2)}) %copy-start) | copy-done | bytes 262168
  2.2 0.0 copy-start.1
  2.2 0.9 %copy-done.1 = bf16[1,128,1024]{2,1,0:T(8,128)(2,1)S(1)} copy-done((bf16[1,128,1024]{2,1,0:T(8,128)(2,1)S(1)}, bf16[1,128,1024]{2,1,0:T(8,128)(2,1)}, u32[]{:S(2)}) %copy-start.1) | copy-done | bytes 262168
  3.2 0.0 copy-start.2
  3.2 0.9 %copy-done.2 = bf16[1,128,1024]{2,1,0:T(8,128)(2,1)S(1)} copy-done((bf16[1,128,1024]{2,1,0:T(8,128)(2,1)S(1)}, bf16[1,128,1024]{2,1,0:T(8,128)(2,1)}, u32[]{:S(2)}) %copy-start.2) | copy-done | bytes 262168
  4.1 0.0 copy-start.3
  4.1 0.9 %copy-done.3 = bf16[1,128,1024]{2,1,0:T(8,128)(2,1)S(1)} copy-done((bf16[1,128,1024]{2,1,0:T(8,128)(2,1)S(1)}, bf16[1,128,1024]{2,1,0:T(8,128)(2,1)}, u32[]{:S(2)}) %copy-start.3) | copy-done | bytes 262168
  5.1 53.0 %shard_map.84 = (bf16[128,1024]{1,0:T(8,128)(2,1)S(1)}, bf16[128,1024]{1,0:T(8,128)(2,1)S(1)}, bf16[128,1024]{1,0:T(8,128)(2,1)S(1)}, bf16[128,1024]{1,0:T(8,128)(2,1)S(1)}) custom-call(s32[1]{0:T(128)S(6)} %copy.13.pad_ref, bf16[1,128,1024]{2,1,0:T(8,128)(2,1)S(1)} %copy-done, bf16[1,128,1024]{2,1,0:T(8,128)(2,1)S(1)} %copy-done.1, ...), custom_call_target="tpu_custom_call" | custom-call | tf_op jit(solution)/shard_map/pallas_call | solution.py:457
  58.1 0.7 %copy.14 = bf16[1,128,1024]{2,1,0:T(8,128)(2,1)} copy(bf16[1,128,1024]{2,1,0:T(8,128)(2,1)S(1)} %bitcast.7) | data formatting | bytes 524288
  58.8 0.7 %copy.15 = bf16[1,128,1024]{2,1,0:T(8,128)(2,1)} copy(bf16[1,128,1024]{2,1,0:T(8,128)(2,1)S(1)} %bitcast.6) | data formatting | bytes 524288
  59.5 0.7 %copy.16 = bf16[1,128,1024]{2,1,0:T(8,128)(2,1)} copy(bf16[1,128,1024]{2,1,0:T(8,128)(2,1)S(1)} %bitcast.5) | data formatting | bytes 524288
  60.2 0.7 %copy.17 = bf16[1,128,1024]{2,1,0:T(8,128)(2,1)} copy(bf16[1,128,1024]{2,1,0:T(8,128)(2,1)S(1)} %bitcast.4) | data formatting | bytes 524288
Async XLA Ops:
  1.3 1.0 %copy-start = (bf16[1,128,1024]{2,1,0:T(8,128)(2,1)S(1)}, bf16[1,128,1024]{2,1,0:T(8,128)(2,1)}, u32[]{:S(2)}) copy-start(bf16[1,128,1024]{2,1,0:T(8,128)(2,1)} %q_ref.1) | copy-start | bytes 786436
  2.2 0.9 %copy-start.1 = (bf16[1,128,1024]{2,1,0:T(8,128)(2,1)S(1)}, bf16[1,128,1024]{2,1,0:T(8,128)(2,1)}, u32[]{:S(2)}) copy-start(bf16[1,128,1024]{2,1,0:T(8,128)(2,1)} %k_ref.1) | copy-start | bytes 786436
  3.2 0.9 %copy-start.2 = (bf16[1,128,1024]{2,1,0:T(8,128)(2,1)S(1)}, bf16[1,128,1024]{2,1,0:T(8,128)(2,1)}, u32[]{:S(2)}) copy-start(bf16[1,128,1024]{2,1,0:T(8,128)(2,1)} %v_ref.1) | copy-start | bytes 786436
  4.1 0.9 %copy-start.3 = (bf16[1,128,1024]{2,1,0:T(8,128)(2,1)S(1)}, bf16[1,128,1024]{2,1,0:T(8,128)(2,1)}, u32[]{:S(2)}) copy-start(bf16[1,128,1024]{2,1,0:T(8,128)(2,1)} %g_ref.1) | copy-start | bytes 786436

commit v3 on v2

--- a/solution.py
+++ b/solution.py
@@ -348,45 +348,7 @@
         def _():
             send_chain(c).start()
 
-    lag = jnp.minimum(CHAIN_LAG * me, chunks)
-
-    def step(t, carry):
-        @pl.when(t < chunks)
-        def _():
-            band(t)
-
-            @pl.when(me == last)
-            def _():
-                send_low_last(t).wait_send()
-
-        @pl.when(t == lag)
-        def _():
-            for k in range(1, n):
-                send_stats(k).wait_recv()
-
-        @pl.when((t >= lag) & (t < lag + chunks))
-        def _():
-            finish(t - lag)
-
-        @pl.when((t >= UP_LAG) & (t < UP_LAG + chunks))
-        def _():
-            @pl.when(me < last - 1)
-            def _():
-                send_up(t - UP_LAG).start()
-
-            @pl.when(me == last - 1)
-            def _():
-                send_up_last(t - UP_LAG).start()
-
-        @pl.when((t >= DOWN_LAG) & (t < DOWN_LAG + chunks) & has_below)
-        def _():
-            send_down(t - DOWN_LAG).start()
-
-        return carry
-
-    lax.fori_loop(0, 2 * chunks, step, 0)
-
-    def combine(c, carry):
+    def combine(c):
         columns = pl.ds(pl.multiple_of(c * PAIR, PAIR), PAIR)
 
         @pl.when(has_below)
@@ -410,9 +372,48 @@
 
         kgrad_ref[:, columns] = own_grad[c, 0].astype(bf16)
         vgrad_ref[:, columns] = own_grad[c, 1].astype(bf16)
+
+    lag = jnp.minimum(CHAIN_LAG * me, chunks)
+
+    def step(t, carry):
+        @pl.when(t < chunks)
+        def _():
+            band(t)
+
+            @pl.when(me == last)
+            def _():
+                send_low_last(t).wait_send()
+
+        @pl.when(t == lag)
+        def _():
+            for k in range(1, n):
+                send_stats(k).wait_recv()
+
+        @pl.when((t >= lag) & (t < lag + chunks))
+        def _():
+            finish(t - lag)
+
+        @pl.when((t >= UP_LAG) & (t < UP_LAG + chunks))
+        def _():
+            @pl.when(me < last - 1)
+            def _():
+                send_up(t - UP_LAG).start()
+
+            @pl.when(me == last - 1)
+            def _():
+                send_up_last(t - UP_LAG).start()
+
+        @pl.when((t >= DOWN_LAG) & (t < DOWN_LAG + chunks) & has_below)
+        def _():
+            send_down(t - DOWN_LAG).start()
+
+        @pl.when(t >= chunks)
+        def _():
+            combine(t - chunks)
+
         return carry
 
-    lax.fori_loop(0, chunks, combine, 0)
+    lax.fori_loop(0, 2 * chunks, step, 0)
 
     def drain(c, carry):
         @pl.when(has_below)
@@ -444,6 +445,17 @@
     lax.fori_loop(0, chunks, drain, 0)
     for k in range(1, n):
         send_stats(k).wait_send()
+
+
+def spill(*refs):
+    sems = refs[8]
+    copies = [
+        pltpu.make_async_copy(refs[k], refs[4 + k].at[0], sems.at[k]) for k in range(4)
+    ]
+    for copy in copies:
+        copy.start()
+    for copy in copies:
+        copy.wait()
 
 
 def per_device(n, query_vectors, key_vectors, value_vectors, out_grad, pad_length):
@@ -457,7 +469,7 @@
     outs = pl.pallas_call(
         functools.partial(kernel, n, rows, chunks),
         out_shape=(out,) * 4,
-        in_specs=[smem] + [pl.BlockSpec(memory_space=pl.ANY)] * 4,
+        in_specs=[smem] + [pl.BlockSpec(memory_space=pltpu.HBM)] * 4,
         out_specs=(vmem,) * 4,
         scratch_shapes=[
             pltpu.VMEM((chunks, 2, all_keys, PAIR), bf16),
@@ -482,10 +494,17 @@
         + [dma((n,))] * 2
         + [dma((chunks,))] * 6,
         compiler_params=pltpu.CompilerParams(
-            collective_id=0, has_side_effects=True, vmem_limit_bytes=48 << 20
+            collective_id=0, has_side_effects=True, vmem_limit_bytes=63 << 20
         ),
     )(pad_length, query_vectors, key_vectors, value_vectors, out_grad)
-    return tuple(array[None] for array in outs)
+    anywhere = pl.BlockSpec(memory_space=pl.ANY)
+    return pl.pallas_call(
+        spill,
+        out_shape=(jax.ShapeDtypeStruct((1, rows, features), bf16),) * 4,
+        in_specs=[vmem] * 4,
+        out_specs=(anywhere,) * 4,
+        scratch_shapes=[dma((4,))],
+    )(*outs)
 
 
 def solution(mesh):

time: 61.2 us -> 58 us (0.948)
  local copies, waits for them, and re-layouts: 6.6 us -> 0 us
  Pallas kernels: 53 us -> 56.4 us
    unnamed x12 -> x0, local copies, waits for them, and re-layouts: 6.6 us -> none
    pallas_call x0 -> x1, Pallas kernels: none -> 2.18 us  [per_device(): pl.pallas_call(spill, out_shape=(jax.ShapeDtypeStruct((1, rows, features)...]
    pallas_call x1, Pallas kernels: 53 us -> 54.2 us  [per_device(): pl.pallas_call(functools.partial(kernel, n, rows, chunks), out_shape=(out...]
where the time goes in v3:
time: 58 us; the launch traced here: 57.7 us
  Pallas kernels  56.4 us (97%)
  between operations  1.29 us (2%)
    pallas_call x1, Pallas kernels, per_device(): pl.pallas_call(functools.partial(kernel, n, rows, chunks), out_shape=(out...  54.2 us
    pallas_call x1, Pallas kernels, per_device(): pl.pallas_call(spill, out_shape=(jax.ShapeDtypeStruct((1, rows, features)...  2.18 us

profile of v3, /device:TPU:28, one launch (start us, length us, event | category | flops | bytes accessed | tf_op | source)
XLA Modules:
  0.0 57.7 jit_solution(17006670906411123837)
XLA Ops:
  1.3 54.2 %shard_map.84 = (bf16[128,1024]{1,0:T(8,128)(2,1)}, bf16[128,1024]{1,0:T(8,128)(2,1)}, bf16[128,1024]{1,0:T(8,128)(2,1)}, bf16[128,1024]{1,0:T(8,128)(2,1)}) custom-call(s32[1]{0:T(128)S(6)} %copy.9.pad_ref, bf16[1,128,1024]{2,1,0:T(8,128)(2,1)} %q_ref.1, bf16[1,128,1024]{2,1,0:T(8,128)(2,1)} %k_ref.1, bf16[1,128,1024]{2,1,0:T(8,128)(2,1)} %v_ref.1, ...), custom_call_target="tpu_custom_call" | custom-call | tf_op jit(solution)/shard_map/pallas_call | solution.py:469
  55.5 2.2 %shard_map.85 = (bf16[1,128,1024]{2,1,0:T(8,128)(2,1)}, bf16[1,128,1024]{2,1,0:T(8,128)(2,1)}, bf16[1,128,1024]{2,1,0:T(8,128)(2,1)}, bf16[1,128,1024]{2,1,0:T(8,128)(2,1)}) custom-call(bf16[128,1024]{1,0:T(8,128)(2,1)} %get-tuple-element.8.refs_0_, bf16[128,1024]{1,0:T(8,128)(2,1)} %get-tuple-element.9.refs_1_, ...), custom_call_target="tpu_custom_call" | custom-call | tf_op jit(solution)/shard_map/pallas_call | solution.py:501
